TPU v7x, 256 devices: a whole 4x4x8 slice. The times are simulated.
256 devices in a mesh: slab: 8 (over z), filt: 32 (over y, x, core).
Axes of the slice: x: 4, y: 4, z: 8, core: 2. Of those that a mesh axis runs over, the one named last changes fastest.
Arguments:
- features: bfloat16 [32, 256, 64, 128], P('slab', 'filt'), may hold values from -6 to 6
- kernel: bfloat16 [3, 3, 3, 256, 256], P(None, None, None, 'filt'), may hold values from -0.078125 to 0.078125
- bias_vector: float32 [256], replicated, may hold values from -0.6 to 0.6
Outputs:
- activated: bfloat16 [32, 256, 64, 128], P('slab', 'filt')
All inputs are finite; a program needn't handle non-finite values.
Results may differ from a plain program's by a relative error of at most 0.005.
Values may be sent and summed in bfloat16 or wider, within the bound.
A program may use at most 128 MiB of HBM per device.

v0:
```python
import jax
import jax.numpy as jnp
from jax import lax
from jax.sharding import PartitionSpec as P

slope = 0.3


def with_halo(array, sides, width):
    for axis, dim in sides:
        devices, length = (lax.axis_size(axis), array.shape[dim])
        up = [(i, (i + 1) % devices) for i in range(devices - 1)]
        down = [(j, i) for i, j in up]
        last = lax.slice_in_dim(array, length - width, length, axis=dim)
        leading = lax.slice_in_dim(array, 0, width, axis=dim)
        before = lax.ppermute(last, axis, up)
        after = lax.ppermute(leading, axis, down)
        array = jnp.concatenate([before, array, after], axis=dim)
    return array


def convolve(volume_piece, taps, y_margin, first_center, out_count):
    in_planes, in_chan, in_rows, in_cols = volume_piece.shape
    out_chan = taps.shape[3]
    out_rows = in_rows - 2 * y_margin
    totals = [
        jnp.zeros((out_chan, out_rows, in_cols), jnp.float32) for slot_index in range(out_count)
    ]
    for plane_index in range(in_planes):
        depth_list = [
            plane_index - (first_center + slot_index) + 1 for slot_index in range(out_count)
        ]
        depth_list = [entry for entry in depth_list if 0 <= entry <= 2]
        depth_low = min(depth_list)
        depth_high = max(depth_list)
        depth_count = depth_high - depth_low + 1
        flat_weight = taps[depth_low : depth_high + 1].reshape(depth_count * 9 * out_chan, in_chan)
        products = jnp.einsum(
            "tc,cyx->tyx",
            flat_weight,
            volume_piece[plane_index],
            preferred_element_type=jnp.float32,
        )
        products = products.reshape(depth_count, 3, 3, out_chan, in_rows, in_cols)
        padded_products = jnp.pad(products, ((0, 0), (0, 0), (0, 0), (0, 0), (1, 1), (1, 1)))
        for slot_index in range(out_count):
            depth_tap = plane_index - (first_center + slot_index) + 1
            if 0 <= depth_tap <= 2:
                for row_tap in range(3):
                    for col_tap in range(3):
                        row_start = y_margin + row_tap
                        totals[slot_index] = (
                            totals[slot_index]
                            + padded_products[
                                depth_tap - depth_low,
                                row_tap,
                                col_tap,
                                :,
                                row_start : row_start + out_rows,
                                col_tap : col_tap + in_cols,
                            ]
                        )
    return jnp.stack(totals)


def finish(convolved, bias_piece):
    shifted = convolved + bias_piece[None, :, None, None]
    return jnp.where(shifted > 0, shifted, slope * shifted).astype(jnp.bfloat16)


def body(features, kernel, bias_vector):
    planes = features.shape[0]
    own_count = kernel.shape[3]
    own_bias = lax.dynamic_slice_in_dim(
        bias_vector, lax.axis_index("filt") * own_count, own_count, 0
    )
    padded = with_halo(features, (("slab", 0),), 1)
    gathered = lax.all_gather(padded, "filt", axis=1, tiled=True)
    convolved = convolve(gathered, kernel, 0, 1, planes)
    return finish(convolved, own_bias)


def solution(mesh):
    placed = (P("slab", "filt", None, None), P(None, None, None, "filt", None), P())
    return jax.shard_map(
        body, mesh=mesh, in_specs=placed, out_specs=P("slab", "filt", None, None), check_vma=False
    )
```

profile of v0, /device:TPU:2, one launch (start us, length us, event | category | flops | bytes accessed | tf_op | source)
XLA Modules:
  0.0 175.0 jit_solution(7436586387113536860)
XLA Ops:
  6.5 0.0 all-gather.2.cloned.1.call-start
  6.5 1.4 copy.4
  8.0 3.8 %collective-permute-start = (bf16[1,8,64,128]{3,1,2,0:T(8,128)(2,1)S(1)}, bf16[1,8,64,128]{3,1,2,0:T(8,128)(2,1)S(1)}, u32[]{:S(2)}, u32[]{:S(2)}) collective-permute-start(bf16[1,8,64,128]{3,1,2,0:T(8,128)(2,1)S(1)} %get-tuple-element.8), channel_id=1, source_target_pairs={{0,32},{32,64},{64,96},{96,128},{128,160},{160,192},{192,224},{1,3... | collective-permute-start | bytes 393224 | tf_op jit(solution)/shard_map/ppermute | solution.py:16
  11.8 1.3 collective-permute-start.1
  13.1 1.4 collective-permute-done
  14.5 4.3 %collective-permute-done.1 = bf16[1,8,64,128]{3,1,2,0:T(8,128)(2,1)S(1)} collective-permute-done((bf16[1,8,64,128]{3,1,2,0:T(8,128)(2,1)S(1)}, bf16[1,8,64,128]{3,1,2,0:T(8,128)(2,1)S(1)}, u32[]{:S(2)}, u32[]{:S(2)}) %collective-permute-start.1) | collective-permute-done | bytes 131104 | tf_op jit(solution)/shard_map/ppermute | solution.py:17
  18.8 1.1 pad_maximum_fusion
  19.9 0.0 all-gather.2.cloned.1.call-update
  19.9 0.8 dynamic_slice.3
  20.7 0.8 fusion.148
  21.5 1.0 fusion.149
  22.4 108.3 %all-gather.2.cloned.1.call-done = bf16[6,256,64,128]{3,1,2,0:T(8,128)(2,1)} async-done(((bf16[6,8,64,128]{3,1,2,0:T(8,128)(2,1)}), bf16[6,256,64,128]{3,1,2,0:T(8,128)(2,1)}) %all-gather.2.cloned.1.call-update) | async-done | bytes 25165840 | tf_op jit(solution)/shard_map/all_gather | solution.py:78
  130.8 3.0 %fusion = f32[64,128,72]{1,2,0:T(8,128)S(1)} fusion(bf16[72,256,1]{1,0,2:T(8,128)(2,1)S(1)} %bitcast.394, bf16[6,256,64,128]{3,1,2,0:T(8,128)(2,1)} %all-gather.2.cloned.1.call-done), kind=kOutput, calls=%fused_computation.97 | convolution fusion | flops 301989888 | bytes 6590464 | tf_op jit(solution)/shard_map/tc,cyx->tyx/dot_general | solution.py:38
  133.8 0.4 copy.23
  134.2 3.0 %fusion.5 = f32[64,128,72]{1,2,0:T(8,128)S(1)} fusion(bf16[72,256,1]{1,0,2:T(8,128)(2,1)S(1)} %bitcast.393, bf16[6,256,64,128]{3,1,2,0:T(8,128)(2,1)} %all-gather.2.cloned.1.call-done), kind=kOutput, calls=%fused_computation.107 | convolution fusion | flops 301989888 | bytes 6590464 | tf_op jit(solution)/shard_map/tc,cyx->tyx/dot_general | solution.py:38
  137.2 1.8 %copy.7 = f32[1,3,3,8,64,128]{5,4,3,2,1,0:T(8,128)} copy(f32[1,3,3,8,64,128]{5,3,2,1,4,0:T(8,128)S(1)} %bitcast.388) | data formatting | bytes 4718592 | tf_op jit(solution)/shard_map/reshape | solution.py:44
  139.0 3.0 %fusion.1 = f32[64,128,144]{1,2,0:T(8,128)S(1)} fusion(bf16[144,256,1]{1,0,2:T(8,128)(2,1)S(1)} %bitcast.392, bf16[6,256,64,128]{3,1,2,0:T(8,128)(2,1)} %all-gather.2.cloned.1.call-done), kind=kOutput, calls=%fused_computation.99 | convolution fusion | flops 603979776 | bytes 8986624 | tf_op jit(solution)/shard_map/tc,cyx->tyx/dot_general | solution.py:38
  142.0 3.6 %copy.19 = f32[2,3,3,8,64,128]{5,4,3,2,1,0:T(8,128)} copy(f32[2,3,3,8,64,128]{5,3,2,1,0,4:T(8,128)S(1)} %bitcast.385) | data formatting | bytes 9437184 | tf_op jit(solution)/shard_map/reshape | solution.py:44
  145.6 3.0 %fusion.4 = f32[64,128,144]{1,2,0:T(8,128)S(1)} fusion(bf16[144,256,1]{1,0,2:T(8,128)(2,1)S(1)} %bitcast.391, bf16[6,256,64,128]{3,1,2,0:T(8,128)(2,1)} %all-gather.2.cloned.1.call-done), kind=kOutput, calls=%fused_computation.105 | convolution fusion | flops 603979776 | bytes 8986624 | tf_op jit(solution)/shard_map/tc,cyx->tyx/dot_general | solution.py:38
  148.6 1.4 copy.9
  150.1 0.0 copy-done
  150.1 3.3 %fusion.3 = f32[64,128,216]{1,2,0:T(8,128)S(1)} fusion(bf16[216,256,1]{1,0,2:T(8,128)(2,1)S(1)} %bitcast.389, bf16[6,256,64,128]{3,1,2,0:T(8,128)(2,1)} %all-gather.2.cloned.1.call-done), kind=kOutput, calls=%fused_computation.103 | convolution fusion | flops 905969664 | bytes 11382784 | tf_op jit(solution)/shard_map/tc,cyx->tyx/dot_general | solution.py:38
  153.4 1.3 copy.11
  154.7 3.3 %fusion.2 = f32[64,128,216]{1,2,0:T(8,128)S(1)} fusion(bf16[216,256,1]{1,0,2:T(8,128)(2,1)S(1)} %bitcast.390, bf16[6,256,64,128]{3,1,2,0:T(8,128)(2,1)} %all-gather.2.cloned.1.call-done), kind=kOutput, calls=%fused_computation.101 | convolution fusion | flops 905969664 | bytes 11382784 | tf_op jit(solution)/shard_map/tc,cyx->tyx/dot_general | solution.py:38
  158.0 0.0 slice-start
  158.0 1.3 copy.15
  159.4 0.0 slice-start.1
  159.4 3.3 %fusion.123 = f32[1,8,64,128]{3,2,1,0:T(8,128)S(1)} fusion(f32[3,3,3,8,64,128]{5,4,3,2,1,0:T(8,128)S(1)} %copy.11, f32[2,3,3,8,64,128]{5,4,3,2,1,0:T(8,128)S(1)} %copy.9, f32[1,3,3,8,64,128]{5,4,3,2,1,0:T(8,128)} %copy.7), kind=kLoop, calls=%fused_computation.228 | loop fusion | flops 1703936 | bytes 15204352 | tf_op jit(solution)/shard_map/add | solution.py:53
  162.7 0.0 slice-done
  162.7 0.0 slice-done.1
  162.7 4.4 %fusion.142 = (f32[1,8,64,128]{3,2,1,0:T(8,128)S(1)}, f32[1,8,64,128]{3,2,1,0:T(8,128)S(1)}, f32[1,8,64,128]{3,2,1,0:T(8,128)S(1)}) fusion(f32[3,3,3,8,64,128]{5,4,3,2,1,0:T(8,128)S(1)} %copy.15, f32[3,3,3,8,64,128]{5,4,3,2,1,0:T(8,128)S(1)} %copy.11, f32[2,3,3,8,64,128]{5,4,3,2,1,0:T(8,128)S(1)} %copy.9, f32[2,3,3,8,64,128]{5,4,3,2,1,0:T(8,128)S(1)} %bitcast.384, ...), kind=kLoop, calls=%fused_computation.247 | loop fusion | flops 5111808 | bytes 29097984 | tf_op jit(solution)/shard_map/add | solution.py:53
  167.1 1.0 fusion.6
  (3 shorter events, 0.0 us)
Async XLA Ops:
  6.5 124.2 %all-gather.2.cloned.1.call-start = ((), (), s32[]{:S(2)}) async-start(), calls=%async_computation | async-start | bytes 25952256 | tf_op jit(solution)/shard_map/all_gather | solution.py:78
  8.0 6.6 %collective-permute-start = (bf16[1,8,64,128]{3,1,2,0:T(8,128)(2,1)S(1)}, bf16[1,8,64,128]{3,1,2,0:T(8,128)(2,1)S(1)}, u32[]{:S(2)}, u32[]{:S(2)}) collective-permute-start(bf16[1,8,64,128]{3,1,2,0:T(8,128)(2,1)S(1)} %get-tuple-element.8), channel_id=1, source_target_pairs={{0,32},{32,64},{64,96},{96,128},{128,160},{160,192},{192,224},{1,3... | collective-permute-start | bytes 393224 | tf_op jit(solution)/shard_map/ppermute | solution.py:16
  11.8 7.0 %collective-permute-start.1 = (bf16[1,8,64,128]{3,1,2,0:T(8,128)(2,1)S(1)}, bf16[1,8,64,128]{3,1,2,0:T(8,128)(2,1)S(1)}, u32[]{:S(2)}, u32[]{:S(2)}) collective-permute-start(bf16[1,8,64,128]{3,1,2,0:T(8,128)(2,1)S(1)} %get-tuple-element.9), channel_id=1, source_target_pairs={{32,0},{64,32},{96,64},{128,96},{160,128},{192,160},{224,192},{33,... | collective-permute-start | bytes 393224 | tf_op jit(solution)/shard_map/ppermute | solution.py:17
  145.6 4.4 %copy-start = (bf16[3,3,3,8,256]{4,3,2,1,0:T(8,128)(2,1)S(1)}, bf16[3,3,3,8,256]{4,3,2,1,0:T(8,128)(2,1)}, u32[]{:S(2)}) copy-start(bf16[3,3,3,8,256]{4,3,2,1,0:T(8,128)(2,1)} %param.4) | copy-start | bytes 331780
  158.0 4.7 %slice-start = ((s8[4718592]{0:T(1024)(128)(4,1)}), s8[524288]{0:T(1024)(128)(4,1)S(1)}, s32[]{:S(2)}) async-start(s8[4718592]{0:T(1024)(128)(4,1)} %bitcast.383), calls=%async_computation.1 | async-start | bytes 1048576
  159.4 3.3 %slice-start.1 = ((s8[4718592]{0:T(1024)(128)(4,1)}), s8[4194304]{0:T(1024)(128)(4,1)S(1)}, s32[]{:S(2)}) async-start(s8[4718592]{0:T(1024)(128)(4,1)} %bitcast.383), calls=%async_computation.2 | async-start | bytes 8388608
Sparse Core Ops, SparseCore 0:
  20.0 110.7 all-gather.1
where the time goes:
time: 177 us; the launch traced here: 175 us
  waiting for transfers between devices  114 us (64%)
  matrix products  18.6 us (11%)
  local copies, waits for them, and re-layouts  13.8 us (8%)
  between operations  13.6 us (8%)
  other arithmetic  9.79 us (6%)
  starting transfers between devices  5.12 us (3%)
    all_gather x1, waiting for transfers between devices, body(): gathered = lax.all_gather(padded, 'filt', axis=1, tiled=True)  108 us
    dot_general x6, matrix products, convolve(): jnp.einsum('tc,cyx->tyx', flat_weight, volume_piece[plane_index], preferr...  18.6 us
    reshape x6, local copies, waits for them, and re-layouts, convolve(): products = products.reshape(depth_count, 3, 3, out_chan, in_rows, in_cols)  9.91 us
    add x2, other arithmetic, convolve(): totals[slot_index]  7.69 us
    ppermute x1, waiting for transfers between devices, with_halo(): after = lax.ppermute(leading, axis, down)  4.3 us
    ppermute x1, starting transfers between devices, with_halo(): before = lax.ppermute(last, axis, up)  3.83 us
  transfers between devices with their start and end apart: 3, of which 3 were waited for; matrix products, arithmetic and copies ran while one was open for 1% of the time, Pallas kernels for 0%

commit v1 on v0

v1 whole, which is shorter than its diff:
```python
import jax
import jax.numpy as jnp
from jax import lax
from jax.experimental import pallas as pl
from jax.experimental.pallas import tpu as pltpu
from jax.sharding import PartitionSpec as P

MESH = pl.DeviceIdType.MESH
SIDE = 4
CHIPS = 16
ROWS = 4
PLANES = 4
ORDER = [3, 4, 5, 0, 1, 2, 6, 7, 8]


def kernel(feat, w, bias, out, turned, vol, taps, acc, ready, column,
           f_s, f_r, x_s, x_r, h_s, h_r, w1_s, w1_r, w2_s, w2_r, o_s, o_r, l_s):
    slab = lax.axis_index("slab")
    filt = lax.axis_index("filt")
    slabs = lax.axis_size("slab")
    chip = filt // 2
    core = filt % 2
    cy = chip // SIDE
    cx = chip % SIDE

    def device(y, x, c):
        return {"filt": (y * SIDE + x) * 2 + c}

    def partner(k):
        y = (cy + k // SIDE) % SIDE
        x = (cx + k % SIDE) % SIDE
        return y, x

    def source(k):
        y = (cy + SIDE - k // SIDE) % SIDE
        x = (cx + SIDE - k % SIDE) % SIDE
        return y * SIDE + x

    barrier = pltpu.get_barrier_semaphore()

    def greet(k, carry):
        y, x = partner(k)
        pl.semaphore_signal(barrier, inc=1, device_id=device(y, x, core), device_id_type=MESH)
        return carry

    lax.fori_loop(1, CHIPS, greet, 0)
    pl.semaphore_signal(barrier, inc=1, device_id=device(cy, cx, 1 - core), device_id_type=MESH)

    for step in (1, slabs - 1):
        pl.semaphore_signal(
            barrier, inc=1, device_id={"slab": (slab + step) % slabs}, device_id_type=MESH
        )

    own_taps = pltpu.make_async_copy(w, taps.at[:, :, cy, cx], l_s.at[0])
    own_taps.start()

    turned[0] = jnp.zeros(turned.shape[1:], turned.dtype)
    turned[turned.shape[0] - 1] = jnp.zeros(turned.shape[1:], turned.dtype)
    for z in range(PLANES):
        turned[1:65, z] = jnp.transpose(feat[z].astype(jnp.float32), (1, 0, 2)).astype(jnp.bfloat16)

    own_feat = pltpu.make_async_copy(
        turned.at[pl.ds(chip * ROWS, ROWS + 2)], vol.at[:, 1:5, chip, core], l_s.at[1]
    )
    own_feat.start()

    wide = jnp.broadcast_to(bias[...].reshape(1, 256), (128, 256))
    column[...] = jnp.transpose(wide, (1, 0)).reshape(CHIPS, 2, 8, 128)

    pl.semaphore_wait(barrier, CHIPS + 2)

    def feat_copy(k):
        y, x = partner(k)
        return pltpu.make_async_remote_copy(
            src_ref=turned.at[pl.ds((y * SIDE + x) * ROWS, ROWS + 2)],
            dst_ref=vol.at[:, 1:5, chip, core],
            send_sem=f_s.at[k], recv_sem=f_r.at[k],
            device_id=device(y, x, core), device_id_type=MESH,
        )

    def feat_arrived(k):
        piece = vol.at[:, 1:5, source(k), core]
        return pltpu.make_async_copy(piece, piece, f_r.at[k])

    def send_feat(k, carry):
        feat_copy(k).start()
        return carry

    lax.fori_loop(1, CHIPS, send_feat, 0)

    def ring(unit, k, phase):
        along_x = (unit % 2 == 0) == (phase == 1)
        if along_x:
            return cy, (cx + k) % SIDE
        return (cy + k) % SIDE, cx

    def ring_source(unit, k, phase):
        along_x = (unit % 2 == 0) == (phase == 1)
        if along_x:
            return cy, (cx + SIDE - k) % SIDE
        return (cy + SIDE - k) % SIDE, cx

    def tap_copy1(unit, k):
        y, x = ring(unit, k, 1)
        return pltpu.make_async_remote_copy(
            src_ref=w.at[unit], dst_ref=taps.at[unit, :, cy, cx],
            send_sem=w1_s.at[unit, k], recv_sem=w1_r.at[unit, k],
            device_id=device(y, x, core), device_id_type=MESH,
        )

    def tap_arrived1(unit, k):
        y, x = ring_source(unit, k, 1)
        piece = taps.at[unit, :, y, x]
        return pltpu.make_async_copy(piece, piece, w1_r.at[unit, k])

    def tap_line(unit, y, x):
        if unit % 2 == 0:
            return taps.at[unit, :, y]
        return taps.at[unit, :, :, x]

    def tap_copy2(unit, k):
        y, x = ring(unit, k, 2)
        line = tap_line(unit, cy, cx)
        return pltpu.make_async_remote_copy(
            src_ref=line, dst_ref=line,
            send_sem=w2_s.at[unit, k], recv_sem=w2_r.at[unit, k],
            device_id=device(y, x, core), device_id_type=MESH,
        )

    def tap_arrived2(unit, k):
        y, x = ring_source(unit, k, 2)
        line = tap_line(unit, y, x)
        return pltpu.make_async_copy(line, line, w2_r.at[unit, k])

    for unit in ORDER:
        for k in range(1, SIDE):
            tap_copy1(unit, k).start()

    own_feat.wait()

    def wait_feat(k, carry):
        feat_arrived(k).wait()
        return carry

    lax.fori_loop(1, CHIPS, wait_feat, 0)

    def across(index, part):
        return pltpu.make_async_remote_copy(
            src_ref=part, dst_ref=part, send_sem=x_s.at[index], recv_sem=x_r.at[index],
            device_id=device(cy, cx, 1 - core), device_id_type=MESH,
        )

    def across_arrived(index, part):
        return pltpu.make_async_copy(part, part, x_r.at[index])

    down = pltpu.make_async_remote_copy(
        src_ref=vol.at[:, 1, :, core], dst_ref=vol.at[:, 5, :, core],
        send_sem=h_s.at[0], recv_sem=h_r.at[0],
        device_id={"slab": slab - 1}, device_id_type=MESH,
    )
    up = pltpu.make_async_remote_copy(
        src_ref=vol.at[:, 4, :, core], dst_ref=vol.at[:, 0, :, core],
        send_sem=h_s.at[1], recv_sem=h_r.at[1],
        device_id={"slab": slab + 1}, device_id_type=MESH,
    )

    @pl.when(slab > 0)
    def _():
        down.start()

    @pl.when(slab < slabs - 1)
    def _():
        up.start()

    middle = across(0, vol.at[:, 1:5, :, core])
    middle.start()

    @pl.when(slab == 0)
    def _():
        for y in range(ROWS + 2):
            vol[y, 0] = jnp.zeros(vol.shape[2:], vol.dtype)

    @pl.when(slab == slabs - 1)
    def _():
        for y in range(ROWS + 2):
            vol[y, 5] = jnp.zeros(vol.shape[2:], vol.dtype)

    own_taps.wait()
    for unit in ORDER:
        for k in range(1, SIDE):
            tap_arrived1(unit, k).wait()
        for k in range(1, SIDE):
            tap_copy2(unit, k).start()

    low = across(1, vol.at[:, 0, :, core])
    high = across(2, vol.at[:, 5, :, core])

    @pl.when(slab > 0)
    def _():
        edge = vol.at[:, 0, :, core]
        pltpu.make_async_copy(edge, edge, h_r.at[1]).wait()
        low.start()

    @pl.when(slab < slabs - 1)
    def _():
        edge = vol.at[:, 5, :, core]
        pltpu.make_async_copy(edge, edge, h_r.at[0]).wait()
        high.start()

    across_arrived(0, vol.at[:, 1:5, :, 1 - core]).wait()

    lane = lax.broadcasted_iota(jnp.int32, (128, 128), 1)

    def out_copy(z, k):
        y, x = partner(k)
        return pltpu.make_async_remote_copy(
            src_ref=ready.at[z, y * SIDE + x], dst_ref=out.at[z, pl.ds(chip * ROWS, ROWS)],
            send_sem=o_s.at[z, k], recv_sem=o_r.at[z, k],
            device_id=device(y, x, core), device_id_type=MESH,
        )

    def out_arrived(z, k):
        piece = out.at[z, pl.ds(source(k) * ROWS, ROWS)]
        return pltpu.make_async_copy(piece, piece, o_r.at[z, k])

    def out_own(z):
        return pltpu.make_async_copy(
            ready.at[z, chip], out.at[z, pl.ds(chip * ROWS, ROWS)], o_s.at[z, 0]
        )

    def finish(z):
        biases = column[:, core].reshape(128, 128)
        for y in range(ROWS):
            part = acc[z, :, y * 128 : (y + 1) * 128]
            before = jnp.where(lane == 0, 0.0, pltpu.roll(part[0:128], 1, 1))
            after = jnp.where(lane == 127, 0.0, pltpu.roll(part[256:384], 127, 1))
            shifted = before + part[128:256] + after + biases
            active = jnp.where(shifted > 0, shifted, 0.3 * shifted)
            ready[z, :, y] = active.reshape(CHIPS, 8, 128).astype(jnp.bfloat16)
        out_own(z).start()

        def send(k, carry):
            out_copy(z, k).start()
            return carry

        lax.fori_loop(1, CHIPS, send, 0)

    for unit in ORDER:
        dz, dy = unit // 3, unit % 3
        if unit == ORDER[3]:
            @pl.when(slab > 0)
            def _():
                across_arrived(1, vol.at[:, 0, :, 1 - core]).wait()

            @pl.when(slab < slabs - 1)
            def _():
                across_arrived(2, vol.at[:, 5, :, 1 - core]).wait()
        for k in range(1, SIDE):
            tap_arrived2(unit, k).wait()

        def plane(z, carry, unit=unit, dz=dz, dy=dy):
            weight = taps[unit].reshape(384, 256)
            lines = [vol[dy + y, z + dz].reshape(256, 128) for y in range(ROWS)]
            product = jnp.dot(weight, jnp.concatenate(lines, axis=1), preferred_element_type=jnp.float32)
            if unit == ORDER[0]:
                acc[z] = product
            else:
                acc[z] += product
            if unit == ORDER[8]:
                finish(z)
            return carry

        lax.fori_loop(0, PLANES, plane, 0)

    def drain_out(i, carry):
        z = i // CHIPS
        k = i % CHIPS

        @pl.when(k == 0)
        def _():
            out_own(z).wait()

        @pl.when(k > 0)
        def _():
            out_copy(z, k).wait_send()
            out_arrived(z, k).wait()

        return carry

    lax.fori_loop(0, PLANES * CHIPS, drain_out, 0)

    def drain_feat(k, carry):
        feat_copy(k).wait_send()
        return carry

    lax.fori_loop(1, CHIPS, drain_feat, 0)
    for unit in ORDER:
        for k in range(1, SIDE):
            tap_copy1(unit, k).wait_send()
            tap_copy2(unit, k).wait_send()
    middle.wait_send()

    @pl.when(slab > 0)
    def _():
        down.wait_send()
        low.wait_send()

    @pl.when(slab < slabs - 1)
    def _():
        up.wait_send()
        high.wait_send()


def body(features, weights, bias_vector):
    DMA = pltpu.SemaphoreType.DMA
    vmem = pl.BlockSpec(memory_space=pltpu.VMEM)
    anywhere = pl.BlockSpec(memory_space=pl.ANY)
    flat = weights.reshape(9, 3, 8, 256)
    got = pl.pallas_call(
        kernel,
        out_shape=jax.ShapeDtypeStruct((PLANES, 64, 8, 128), jnp.bfloat16),
        in_specs=[vmem, anywhere, vmem],
        out_specs=anywhere,
        scratch_shapes=[
            pltpu.VMEM((66, PLANES, 8, 128), jnp.bfloat16),
            pltpu.VMEM((ROWS + 2, PLANES + 2, CHIPS, 2, 8, 128), jnp.bfloat16),
            pltpu.VMEM((9, 3, SIDE, SIDE, 8, 256), jnp.bfloat16),
            pltpu.VMEM((PLANES, 384, ROWS * 128), jnp.float32),
            pltpu.VMEM((PLANES, CHIPS, ROWS, 8, 128), jnp.bfloat16),
            pltpu.VMEM((CHIPS, 2, 8, 128), jnp.float32),
            DMA((CHIPS,)), DMA((CHIPS,)),
            DMA((3,)), DMA((3,)),
            DMA((2,)), DMA((2,)),
            DMA((9, SIDE)), DMA((9, SIDE)),
            DMA((9, SIDE)), DMA((9, SIDE)),
            DMA((PLANES, CHIPS)), DMA((PLANES, CHIPS)),
            DMA((2,)),
        ],
        compiler_params=pltpu.CompilerParams(
            collective_id=0, has_side_effects=True, vmem_limit_bytes=40 * 1024 * 1024
        ),
    )(features, flat, bias_vector)
    return got.transpose(0, 2, 1, 3)


def solution(mesh):
    placed = (P("slab", "filt", None, None), P(None, None, None, "filt", None), P())
    return jax.shard_map(
        body, mesh=mesh, in_specs=placed, out_specs=P("slab", "filt", None, None), check_vma=False
    )
```

time: 177 us -> 48.6 us (0.27); the launches traced: 175 us -> 48.4 us
  waiting for transfers between devices: 114 us -> 0 us
  Pallas kernels: 0 us -> 44.9 us
  matrix products: 18.6 us -> 0 us
  between operations: 13.6 us -> 0.01 us
  local copies, waits for them, and re-layouts: 13.8 us -> 3.53 us
  other arithmetic: 9.79 us -> 0 us
  starting transfers between devices: 5.12 us -> 0 us
    all_gather x1 -> x0, waiting for transfers between devices: 108 us -> none  [body(): gathered = lax.all_gather(padded, 'filt', axis=1, tiled=True)]
    pallas_call x0 -> x1, Pallas kernels: none -> 44.9 us  [body(): pl.pallas_call(kernel, out_shape=jax.ShapeDtypeStruct((PLANES, 64, 8, 128...]
    dot_general x6 -> x0, matrix products: 18.6 us -> none  [convolve(): jnp.einsum('tc,cyx->tyx', flat_weight, volume_piece[plane_index], preferr...]
    reshape x6 -> x0, local copies, waits for them, and re-layouts: 9.91 us -> none  [convolve(): products = products.reshape(depth_count, 3, 3, out_chan, in_rows, in_cols)]
    add x2 -> x0, other arithmetic: 7.69 us -> none  [convolve(): totals[slot_index]]
    ppermute x2 -> x0, waiting for transfers between devices: 5.73 us -> none  [the longest x1 4.3 us: with_halo(): after = lax.ppermute(leading, axis, down)]
    ppermute x2 -> x0, starting transfers between devices: 5.12 us -> none  [the longest x1 3.83 us: with_halo(): before = lax.ppermute(last, axis, up)]
    slice x3 -> x0, local copies, waits for them, and re-layouts: 1.78 us -> none  [the longest x2 1.76 us: convolve(): taps[depth_low:depth_high + 1].reshape(depth_count * 9 * out_chan, in_chan)]
  transfers between devices with their start and end apart: 3 -> 0, of which waited for: 3 -> 0; matrix products, arithmetic and copies ran while one was open for 1% -> 0% of each run, Pallas kernels for 0% -> 0%
where the time goes in v1:
time: 48.6 us; the launch traced here: 48.4 us
  Pallas kernels  44.9 us (92%)
  local copies, waits for them, and re-layouts  3.53 us (7%)
    pallas_call x1, Pallas kernels, body(): pl.pallas_call(kernel, out_shape=jax.ShapeDtypeStruct((PLANES, 64, 8, 128...  44.9 us
    unnamed x6, local copies, waits for them, and re-layouts  2.62 us

profile of v1, /device:TPU:2, one launch (start us, length us, event | category | flops | bytes accessed | tf_op | source)
XLA Modules:
  0.0 48.4 jit_solution(11940700719172987045)
XLA Ops:
  0.0 0.0 copy-start.2
  0.0 0.7 %copy-done.2 = f32[256]{0:T(256)S(1)} copy-done((f32[256]{0:T(256)S(1)}, f32[256]{0:T(256)}, u32[]{:S(2)}) %copy-start.2) | copy-done | bytes 1048
  0.7 0.0 copy-start
  0.7 1.0 %copy-done = bf16[4,8,64,128]{3,2,1,0:T(8,128)(2,1)S(1)} copy-done((bf16[4,8,64,128]{3,2,1,0:T(8,128)(2,1)S(1)}, bf16[4,8,64,128]{3,2,1,0:T(8,128)(2,1)}, u32[]{:S(2)}) %copy-start) | copy-done | bytes 524312
  1.7 0.0 copy-start.1
  1.7 0.9 %copy-done.1 = bf16[3,3,3,8,256]{4,3,2,1,0:T(8,128)(2,1)S(1)} copy-done((bf16[3,3,3,8,256]{4,3,2,1,0:T(8,128)(2,1)S(1)}, bf16[3,3,3,8,256]{4,3,2,1,0:T(8,128)(2,1)}, u32[]{:S(2)}) %copy-start.1) | copy-done | bytes 110616
  2.6 44.9 %shard_map.37 = bf16[4,64,8,128]{3,2,1,0:T(8,128)(2,1)S(1)} custom-call(bf16[4,8,64,128]{3,2,1,0:T(8,128)(2,1)S(1)} %copy-done, bf16[9,3,8,256]{3,2,1,0:T(8,128)(2,1)S(1)} %bitcast.3, f32[256]{0:T(256)S(1)} %copy-done.2), custom_call_target="tpu_custom_call" | custom-call | tf_op jit(solution)/shard_map/pallas_call | solution.py:319
  47.5 0.9 %copy.4 = bf16[4,8,64,128]{3,2,1,0:T(8,128)(2,1)} copy(bf16[4,8,64,128]{3,1,2,0:T(8,128)(2,1)S(1)} %bitcast.2) | data formatting | bytes 1048576 | tf_op jit(solution)/shard_map/transpose | solution.py:343
Async XLA Ops:
  0.0 0.7 %copy-start.2 = (f32[256]{0:T(256)S(1)}, f32[256]{0:T(256)}, u32[]{:S(2)}) copy-start(f32[256]{0:T(256)} %bias.1) | copy-start | bytes 3076
  0.7 1.0 %copy-start = (bf16[4,8,64,128]{3,2,1,0:T(8,128)(2,1)S(1)}, bf16[4,8,64,128]{3,2,1,0:T(8,128)(2,1)}, u32[]{:S(2)}) copy-start(bf16[4,8,64,128]{3,2,1,0:T(8,128)(2,1)} %feat.1) | copy-start | bytes 1572868
  1.7 0.9 %copy-start.1 = (bf16[3,3,3,8,256]{4,3,2,1,0:T(8,128)(2,1)S(1)}, bf16[3,3,3,8,256]{4,3,2,1,0:T(8,128)(2,1)}, u32[]{:S(2)}) copy-start(bf16[3,3,3,8,256]{4,3,2,1,0:T(8,128)(2,1)} %param.4) | copy-start | bytes 331780

commit v2 on v1

--- a/solution.py
+++ b/solution.py
@@ -10,11 +10,14 @@
 CHIPS = 16
 ROWS = 4
 PLANES = 4
-ORDER = [3, 4, 5, 0, 1, 2, 6, 7, 8]
-
-
-def kernel(feat, w, bias, out, turned, vol, taps, acc, ready, column,
-           f_s, f_r, x_s, x_r, h_s, h_r, w1_s, w1_r, w2_s, w2_r, o_s, o_r, l_s):
+COUPLES = ()
+COMMON = (3, 4, 5, 1, 7, 0, 2, 6, 8)
+OWN = len(COUPLES) + len(COMMON)
+X_FIRST = (0, 2, 4, 6, 8)
+
+
+def kernel(feat_hbm, w, bias_hbm, out, feat, bias, turned, vol, taps, acc, ready, column,
+           f_s, f_r, x_s, x_r, h_s, h_r, w1_s, w1_r, w2_s, w2_r, z_s, z_r, o_s, o_r, l_s):
     slab = lax.axis_index("slab")
     filt = lax.axis_index("filt")
     slabs = lax.axis_size("slab")
@@ -51,19 +54,46 @@
             barrier, inc=1, device_id={"slab": (slab + step) % slabs}, device_id_type=MESH
         )
 
-    own_taps = pltpu.make_async_copy(w, taps.at[:, :, cy, cx], l_s.at[0])
-    own_taps.start()
+    odd = slab % 2
+
+    def pair(i, parity):
+        if i >= len(COUPLES):
+            return COMMON[i - len(COUPLES)]
+        first, second = COUPLES[i]
+        return first + parity * (second - first)
+
+    take_feat = pltpu.make_async_copy(feat_hbm, feat, l_s.at[0])
+    take_feat.start()
+    take_bias = pltpu.make_async_copy(bias_hbm, bias, l_s.at[1])
+    take_bias.start()
+    own_taps = []
+    for i in range(OWN):
+        unit = pair(i, odd)
+        own_taps.append(pltpu.make_async_copy(w.at[unit], taps.at[unit, :, cy, cx], l_s.at[3 + i]))
+        own_taps[i].start()
+
+    @pl.when(slab == 0)
+    def _():
+        for y in range(ROWS + 2):
+            vol[y, 0] = jnp.zeros(vol.shape[2:], vol.dtype)
+
+    @pl.when(slab == slabs - 1)
+    def _():
+        for y in range(ROWS + 2):
+            vol[y, 5] = jnp.zeros(vol.shape[2:], vol.dtype)
 
     turned[0] = jnp.zeros(turned.shape[1:], turned.dtype)
     turned[turned.shape[0] - 1] = jnp.zeros(turned.shape[1:], turned.dtype)
+    take_feat.wait()
     for z in range(PLANES):
         turned[1:65, z] = jnp.transpose(feat[z].astype(jnp.float32), (1, 0, 2)).astype(jnp.bfloat16)
 
     own_feat = pltpu.make_async_copy(
-        turned.at[pl.ds(chip * ROWS, ROWS + 2)], vol.at[:, 1:5, chip, core], l_s.at[1]
+        turned.at[pl.ds(chip * ROWS, ROWS + 2)], vol.at[:, 1:5, chip, core], l_s.at[2]
     )
     own_feat.start()
 
+    take_bias.wait()
     wide = jnp.broadcast_to(bias[...].reshape(1, 256), (128, 256))
     column[...] = jnp.transpose(wide, (1, 0)).reshape(CHIPS, 2, 8, 128)
 
@@ -86,55 +116,74 @@
         feat_copy(k).start()
         return carry
 
+    def ring(i, k, phase, sign):
+        step = k if sign > 0 else SIDE - k
+        if (i in X_FIRST) == (phase == 1):
+            return cy, (cx + step) % SIDE
+        return (cy + step) % SIDE, cx
+
+    def tap_copy1(i, k):
+        y, x = ring(i, k, 1, 1)
+        return pltpu.make_async_remote_copy(
+            src_ref=w.at[pair(i, odd)], dst_ref=taps.at[pair(i, odd), :, cy, cx],
+            send_sem=w1_s.at[i, k], recv_sem=w1_r.at[i, k],
+            device_id=device(y, x, core), device_id_type=MESH,
+        )
+
+    def tap_arrived1(i, k):
+        y, x = ring(i, k, 1, -1)
+        piece = taps.at[pair(i, odd), :, y, x]
+        return pltpu.make_async_copy(piece, piece, w1_r.at[i, k])
+
+    def tap_line(i, y, x):
+        if i in X_FIRST:
+            return taps.at[pair(i, odd), :, y]
+        return taps.at[pair(i, odd), :, :, x]
+
+    def tap_copy2(i, k):
+        y, x = ring(i, k, 2, 1)
+        line = tap_line(i, cy, cx)
+        return pltpu.make_async_remote_copy(
+            src_ref=line, dst_ref=line, send_sem=w2_s.at[i, k], recv_sem=w2_r.at[i, k],
+            device_id=device(y, x, core), device_id_type=MESH,
+        )
+
+    def tap_arrived2(i, k):
+        y, x = ring(i, k, 2, -1)
+        line = tap_line(i, y, x)
+        return pltpu.make_async_copy(line, line, w2_r.at[i, k])
+
+    def tap_copy3(c):
+        unit = taps.at[pair(c, odd)]
+        step = 1 if c == 0 else slabs - 1
+        return pltpu.make_async_remote_copy(
+            src_ref=unit, dst_ref=unit, send_sem=z_s.at[c], recv_sem=z_r.at[c],
+            device_id={"slab": (slab + step) % slabs}, device_id_type=MESH,
+        )
+
+    def tap_arrived3(c):
+        unit = taps.at[pair(c, 1 - odd)]
+        return pltpu.make_async_copy(unit, unit, z_r.at[c])
+
+    def second_phase(which):
+        for i in which:
+            own_taps[i].wait()
+            for k in range(1, SIDE):
+                tap_arrived1(i, k).wait()
+            for k in range(1, SIDE):
+                tap_copy2(i, k).start()
+
+    def third_phase():
+        for c in range(len(COUPLES)):
+            for k in range(1, SIDE):
+                tap_arrived2(c, k).wait()
+            tap_copy3(c).start()
+
     lax.fori_loop(1, CHIPS, send_feat, 0)
-
-    def ring(unit, k, phase):
-        along_x = (unit % 2 == 0) == (phase == 1)
-        if along_x:
-            return cy, (cx + k) % SIDE
-        return (cy + k) % SIDE, cx
-
-    def ring_source(unit, k, phase):
-        along_x = (unit % 2 == 0) == (phase == 1)
-        if along_x:
-            return cy, (cx + SIDE - k) % SIDE
-        return (cy + SIDE - k) % SIDE, cx
-
-    def tap_copy1(unit, k):
-        y, x = ring(unit, k, 1)
-        return pltpu.make_async_remote_copy(
-            src_ref=w.at[unit], dst_ref=taps.at[unit, :, cy, cx],
-            send_sem=w1_s.at[unit, k], recv_sem=w1_r.at[unit, k],
-            device_id=device(y, x, core), device_id_type=MESH,
-        )
-
-    def tap_arrived1(unit, k):
-        y, x = ring_source(unit, k, 1)
-        piece = taps.at[unit, :, y, x]
-        return pltpu.make_async_copy(piece, piece, w1_r.at[unit, k])
-
-    def tap_line(unit, y, x):
-        if unit % 2 == 0:
-            return taps.at[unit, :, y]
-        return taps.at[unit, :, :, x]
-
-    def tap_copy2(unit, k):
-        y, x = ring(unit, k, 2)
-        line = tap_line(unit, cy, cx)
-        return pltpu.make_async_remote_copy(
-            src_ref=line, dst_ref=line,
-            send_sem=w2_s.at[unit, k], recv_sem=w2_r.at[unit, k],
-            device_id=device(y, x, core), device_id_type=MESH,
-        )
-
-    def tap_arrived2(unit, k):
-        y, x = ring_source(unit, k, 2)
-        line = tap_line(unit, y, x)
-        return pltpu.make_async_copy(line, line, w2_r.at[unit, k])
-
-    for unit in ORDER:
+    for i in range(OWN):
         for k in range(1, SIDE):
-            tap_copy1(unit, k).start()
+            tap_copy1(i, k).start()
+    second_phase(range(OWN))
 
     own_feat.wait()
 
@@ -174,39 +223,10 @@
 
     middle = across(0, vol.at[:, 1:5, :, core])
     middle.start()
-
-    @pl.when(slab == 0)
-    def _():
-        for y in range(ROWS + 2):
-            vol[y, 0] = jnp.zeros(vol.shape[2:], vol.dtype)
-
-    @pl.when(slab == slabs - 1)
-    def _():
-        for y in range(ROWS + 2):
-            vol[y, 5] = jnp.zeros(vol.shape[2:], vol.dtype)
-
-    own_taps.wait()
-    for unit in ORDER:
-        for k in range(1, SIDE):
-            tap_arrived1(unit, k).wait()
-        for k in range(1, SIDE):
-            tap_copy2(unit, k).start()
+    third_phase()
 
     low = across(1, vol.at[:, 0, :, core])
     high = across(2, vol.at[:, 5, :, core])
-
-    @pl.when(slab > 0)
-    def _():
-        edge = vol.at[:, 0, :, core]
-        pltpu.make_async_copy(edge, edge, h_r.at[1]).wait()
-        low.start()
-
-    @pl.when(slab < slabs - 1)
-    def _():
-        edge = vol.at[:, 5, :, core]
-        pltpu.make_async_copy(edge, edge, h_r.at[0]).wait()
-        high.start()
-
     across_arrived(0, vol.at[:, 1:5, :, 1 - core]).wait()
 
     lane = lax.broadcasted_iota(jnp.int32, (128, 128), 1)
@@ -245,9 +265,42 @@
 
         lax.fori_loop(1, CHIPS, send, 0)
 
-    for unit in ORDER:
+    def multiply(unit, first=False, last=False):
         dz, dy = unit // 3, unit % 3
-        if unit == ORDER[3]:
+        lines = [
+            vol[dy + y, z + dz].reshape(256, 128) for z in range(PLANES) for y in range(ROWS)
+        ]
+        product = jnp.dot(
+            taps[unit].reshape(384, 256),
+            jnp.concatenate(lines, axis=1),
+            preferred_element_type=jnp.float32,
+        )
+        for z in range(PLANES):
+            part = product[:, z * ROWS * 128 : (z + 1) * ROWS * 128]
+            if first:
+                acc[z] = part
+            else:
+                acc[z] += part
+            if last:
+                finish(z)
+
+    for i in range(len(COUPLES), OWN):
+        for k in range(1, SIDE):
+            tap_arrived2(i, k).wait()
+        if i == len(COUPLES) + 1:
+            @pl.when(slab > 0)
+            def _():
+                edge = vol.at[:, 0, :, core]
+                pltpu.make_async_copy(edge, edge, h_r.at[1]).wait()
+                low.start()
+
+            @pl.when(slab < slabs - 1)
+            def _():
+                edge = vol.at[:, 5, :, core]
+                pltpu.make_async_copy(edge, edge, h_r.at[0]).wait()
+                high.start()
+
+        if i == len(COUPLES) + 3:
             @pl.when(slab > 0)
             def _():
                 across_arrived(1, vol.at[:, 0, :, 1 - core]).wait()
@@ -255,22 +308,12 @@
             @pl.when(slab < slabs - 1)
             def _():
                 across_arrived(2, vol.at[:, 5, :, 1 - core]).wait()
-        for k in range(1, SIDE):
-            tap_arrived2(unit, k).wait()
-
-        def plane(z, carry, unit=unit, dz=dz, dy=dy):
-            weight = taps[unit].reshape(384, 256)
-            lines = [vol[dy + y, z + dz].reshape(256, 128) for y in range(ROWS)]
-            product = jnp.dot(weight, jnp.concatenate(lines, axis=1), preferred_element_type=jnp.float32)
-            if unit == ORDER[0]:
-                acc[z] = product
-            else:
-                acc[z] += product
-            if unit == ORDER[8]:
-                finish(z)
-            return carry
-
-        lax.fori_loop(0, PLANES, plane, 0)
+
+        multiply(pair(i, 0), first=i == len(COUPLES), last=i == OWN - 1)
+    for c in range(len(COUPLES)):
+        tap_arrived3(c).wait()
+        multiply(COUPLES[c][0])
+        multiply(COUPLES[c][1], last=c == len(COUPLES) - 1)
 
     def drain_out(i, carry):
         z = i // CHIPS
@@ -294,10 +337,12 @@
         return carry
 
     lax.fori_loop(1, CHIPS, drain_feat, 0)
-    for unit in ORDER:
+    for i in range(OWN):
         for k in range(1, SIDE):
-            tap_copy1(unit, k).wait_send()
-            tap_copy2(unit, k).wait_send()
+            tap_copy1(i, k).wait_send()
+            tap_copy2(i, k).wait_send()
+    for c in range(len(COUPLES)):
+        tap_copy3(c).wait_send()
     middle.wait_send()
 
     @pl.when(slab > 0)
@@ -313,15 +358,17 @@
 
 def body(features, weights, bias_vector):
     DMA = pltpu.SemaphoreType.DMA
-    vmem = pl.BlockSpec(memory_space=pltpu.VMEM)
+    hbm = pl.BlockSpec(memory_space=pltpu.HBM)
     anywhere = pl.BlockSpec(memory_space=pl.ANY)
     flat = weights.reshape(9, 3, 8, 256)
     got = pl.pallas_call(
         kernel,
         out_shape=jax.ShapeDtypeStruct((PLANES, 64, 8, 128), jnp.bfloat16),
-        in_specs=[vmem, anywhere, vmem],
+        in_specs=[hbm, hbm, hbm],
         out_specs=anywhere,
         scratch_shapes=[
+            pltpu.VMEM((PLANES, 8, 64, 128), jnp.bfloat16),
+            pltpu.VMEM((256,), jnp.float32),
             pltpu.VMEM((66, PLANES, 8, 128), jnp.bfloat16),
             pltpu.VMEM((ROWS + 2, PLANES + 2, CHIPS, 2, 8, 128), jnp.bfloat16),
             pltpu.VMEM((9, 3, SIDE, SIDE, 8, 256), jnp.bfloat16),
@@ -331,15 +378,16 @@
             DMA((CHIPS,)), DMA((CHIPS,)),
             DMA((3,)), DMA((3,)),
             DMA((2,)), DMA((2,)),
-            DMA((9, SIDE)), DMA((9, SIDE)),
-            DMA((9, SIDE)), DMA((9, SIDE)),
+            DMA((OWN, SIDE)), DMA((OWN, SIDE)),
+            DMA((OWN, SIDE)), DMA((OWN, SIDE)),
+            DMA((1,)), DMA((1,)),
             DMA((PLANES, CHIPS)), DMA((PLANES, CHIPS)),
-            DMA((2,)),
+            DMA((3 + OWN,)),
         ],
         compiler_params=pltpu.CompilerParams(
             collective_id=0, has_side_effects=True, vmem_limit_bytes=40 * 1024 * 1024
         ),
-    )(features, flat, bias_vector)
+    )(*[pltpu.with_memory_space_constraint(a, pltpu.HBM) for a in (features, flat, bias_vector)])
     return got.transpose(0, 2, 1, 3)
 
 

time: 48.6 us -> 45 us (0.926)
  the two profiles are of different devices: /device:TPU:2 before, /device:TPU:33 now
where the time goes in v2:
time: 45 us; the launch traced here: 44.9 us
  Pallas kernels  44 us (98%)
  local copies, waits for them, and re-layouts  0.91 us (2%)
    pallas_call x1, Pallas kernels, body(): pl.pallas_call(kernel, out_shape=jax.ShapeDtypeStruct((PLANES, 64, 8, 128...  44 us
    transpose x1, local copies, waits for them, and re-layouts, body(): return got.transpose(0, 2, 1, 3)  0.91 us

profile of v2, /device:TPU:33, one launch (start us, length us, event | category | flops | bytes accessed | tf_op | source)
XLA Modules:
  0.0 44.9 jit_solution(16632981383793534290)
XLA Ops:
  0.0 44.0 %shard_map.37 = bf16[4,64,8,128]{3,2,1,0:T(8,128)(2,1)S(1)} custom-call(bf16[4,8,64,128]{3,2,1,0:T(8,128)(2,1)} %feat_hbm.1, bf16[9,3,8,256]{3,2,1,0:T(8,128)(2,1)} %bitcast.3, f32[256]{0:T(256)} %bias_hbm.1), custom_call_target="tpu_custom_call" | custom-call | tf_op jit(solution)/shard_map/pallas_call | solution.py:364
  44.0 0.9 %copy.4 = bf16[4,8,64,128]{3,2,1,0:T(8,128)(2,1)} copy(bf16[4,8,64,128]{3,1,2,0:T(8,128)(2,1)S(1)} %bitcast.2) | data formatting | bytes 1048576 | tf_op jit(solution)/shard_map/transpose | solution.py:391

commit v3 on v2

--- a/solution.py
+++ b/solution.py
@@ -10,10 +10,12 @@
 CHIPS = 16
 ROWS = 4
 PLANES = 4
-COUPLES = ()
-COMMON = (3, 4, 5, 1, 7, 0, 2, 6, 8)
+COUPLES = ((0, 6), (2, 8))
+COMMON = (3, 4, 5, 1, 7)
 OWN = len(COUPLES) + len(COMMON)
-X_FIRST = (0, 2, 4, 6, 8)
+X_FIRST = (0, 2, 4, 6)
+PARTS = (0, 3, slice(1, 3))
+PLACES = (1, 4, slice(2, 4))
 
 
 def kernel(feat_hbm, w, bias_hbm, out, feat, bias, turned, vol, taps, acc, ready, column,
@@ -99,22 +101,29 @@
 
     pl.semaphore_wait(barrier, CHIPS + 2)
 
-    def feat_copy(k):
+    def feat_copy(g, k):
         y, x = partner(k)
         return pltpu.make_async_remote_copy(
-            src_ref=turned.at[pl.ds((y * SIDE + x) * ROWS, ROWS + 2)],
-            dst_ref=vol.at[:, 1:5, chip, core],
-            send_sem=f_s.at[k], recv_sem=f_r.at[k],
+            src_ref=turned.at[pl.ds((y * SIDE + x) * ROWS, ROWS + 2), PARTS[g]],
+            dst_ref=vol.at[:, PLACES[g], chip, core],
+            send_sem=f_s.at[g, k], recv_sem=f_r.at[g, k],
             device_id=device(y, x, core), device_id_type=MESH,
         )
 
-    def feat_arrived(k):
-        piece = vol.at[:, 1:5, source(k), core]
-        return pltpu.make_async_copy(piece, piece, f_r.at[k])
-
-    def send_feat(k, carry):
-        feat_copy(k).start()
-        return carry
+    def send_feat(g):
+        def send(k, carry):
+            feat_copy(g, k).start()
+            return carry
+
+        lax.fori_loop(1, CHIPS, send, 0)
+
+    def wait_feat(g):
+        def wait(k, carry):
+            piece = vol.at[:, PLACES[g], source(k), core]
+            pltpu.make_async_copy(piece, piece, f_r.at[g, k]).wait()
+            return carry
+
+        lax.fori_loop(1, CHIPS, wait, 0)
 
     def ring(i, k, phase, sign):
         step = k if sign > 0 else SIDE - k
@@ -178,20 +187,6 @@
             for k in range(1, SIDE):
                 tap_arrived2(c, k).wait()
             tap_copy3(c).start()
-
-    lax.fori_loop(1, CHIPS, send_feat, 0)
-    for i in range(OWN):
-        for k in range(1, SIDE):
-            tap_copy1(i, k).start()
-    second_phase(range(OWN))
-
-    own_feat.wait()
-
-    def wait_feat(k, carry):
-        feat_arrived(k).wait()
-        return carry
-
-    lax.fori_loop(1, CHIPS, wait_feat, 0)
 
     def across(index, part):
         return pltpu.make_async_remote_copy(
@@ -213,21 +208,41 @@
         device_id={"slab": slab + 1}, device_id_type=MESH,
     )
 
+    send_feat(0)
+    send_feat(1)
+    for i in range(OWN):
+        for k in range(1, SIDE):
+            tap_copy1(i, k).start()
+    send_feat(2)
+    own_feat.wait()
+    wait_feat(0)
+
     @pl.when(slab > 0)
     def _():
         down.start()
 
+    bottom = across(0, vol.at[:, 1, :, core])
+    bottom.start()
+    wait_feat(1)
+
     @pl.when(slab < slabs - 1)
     def _():
         up.start()
 
-    middle = across(0, vol.at[:, 1:5, :, core])
+    top = across(3, vol.at[:, 4, :, core])
+    top.start()
+    second_phase(range(len(COUPLES)))
+    second_phase(range(len(COUPLES), OWN))
+    wait_feat(2)
+    middle = across(4, vol.at[:, 2:4, :, core])
     middle.start()
     third_phase()
 
     low = across(1, vol.at[:, 0, :, core])
     high = across(2, vol.at[:, 5, :, core])
-    across_arrived(0, vol.at[:, 1:5, :, 1 - core]).wait()
+    across_arrived(0, vol.at[:, 1, :, 1 - core]).wait()
+    across_arrived(3, vol.at[:, 4, :, 1 - core]).wait()
+    across_arrived(4, vol.at[:, 2:4, :, 1 - core]).wait()
 
     lane = lax.broadcasted_iota(jnp.int32, (128, 128), 1)
 
@@ -309,11 +324,12 @@
             def _():
                 across_arrived(2, vol.at[:, 5, :, 1 - core]).wait()
 
+        if i == OWN - 1:
+            for c in range(len(COUPLES)):
+                tap_arrived3(c).wait()
+                multiply(COUPLES[c][0])
+                multiply(COUPLES[c][1])
         multiply(pair(i, 0), first=i == len(COUPLES), last=i == OWN - 1)
-    for c in range(len(COUPLES)):
-        tap_arrived3(c).wait()
-        multiply(COUPLES[c][0])
-        multiply(COUPLES[c][1], last=c == len(COUPLES) - 1)
 
     def drain_out(i, carry):
         z = i // CHIPS
@@ -333,7 +349,8 @@
     lax.fori_loop(0, PLANES * CHIPS, drain_out, 0)
 
     def drain_feat(k, carry):
-        feat_copy(k).wait_send()
+        for g in range(len(PARTS)):
+            feat_copy(g, k).wait_send()
         return carry
 
     lax.fori_loop(1, CHIPS, drain_feat, 0)
@@ -343,6 +360,8 @@
             tap_copy2(i, k).wait_send()
     for c in range(len(COUPLES)):
         tap_copy3(c).wait_send()
+    bottom.wait_send()
+    top.wait_send()
     middle.wait_send()
 
     @pl.when(slab > 0)
@@ -375,12 +394,12 @@
             pltpu.VMEM((PLANES, 384, ROWS * 128), jnp.float32),
             pltpu.VMEM((PLANES, CHIPS, ROWS, 8, 128), jnp.bfloat16),
             pltpu.VMEM((CHIPS, 2, 8, 128), jnp.float32),
-            DMA((CHIPS,)), DMA((CHIPS,)),
-            DMA((3,)), DMA((3,)),
+            DMA((len(PARTS), CHIPS)), DMA((len(PARTS), CHIPS)),
+            DMA((5,)), DMA((5,)),
             DMA((2,)), DMA((2,)),
             DMA((OWN, SIDE)), DMA((OWN, SIDE)),
             DMA((OWN, SIDE)), DMA((OWN, SIDE)),
-            DMA((1,)), DMA((1,)),
+            DMA((len(COUPLES),)), DMA((len(COUPLES),)),
             DMA((PLANES, CHIPS)), DMA((PLANES, CHIPS)),
             DMA((3 + OWN,)),
         ],

time: 45 us -> 43.9 us (0.976)
  the two profiles are of different devices: /device:TPU:33 before, /device:TPU:2 now
where the time goes in v3:
time: 43.9 us; the launch traced here: 43.6 us
  Pallas kernels  42.7 us (97%)
  local copies, waits for them, and re-layouts  0.91 us (2%)
    pallas_call x1, Pallas kernels, body(): pl.pallas_call(kernel, out_shape=jax.ShapeDtypeStruct((PLANES, 64, 8, 128...  42.7 us
    transpose x1, local copies, waits for them, and re-layouts, body(): return got.transpose(0, 2, 1, 3)  0.91 us

profile of v3, /device:TPU:2, one launch (start us, length us, event | category | flops | bytes accessed | tf_op | source)
XLA Modules:
  0.0 43.6 jit_solution(2757544084552152310)
XLA Ops:
  0.0 42.7 %shard_map.37 = bf16[4,64,8,128]{3,2,1,0:T(8,128)(2,1)S(1)} custom-call(bf16[4,8,64,128]{3,2,1,0:T(8,128)(2,1)} %feat_hbm.1, bf16[9,3,8,256]{3,2,1,0:T(8,128)(2,1)} %bitcast.3, f32[256]{0:T(256)} %bias_hbm.1), custom_call_target="tpu_custom_call" | custom-call | tf_op jit(solution)/shard_map/pallas_call | solution.py:383
  42.7 0.9 %copy.4 = bf16[4,8,64,128]{3,2,1,0:T(8,128)(2,1)} copy(bf16[4,8,64,128]{3,1,2,0:T(8,128)(2,1)S(1)} %bitcast.2) | data formatting | bytes 1048576 | tf_op jit(solution)/shard_map/transpose | solution.py:410

commit v4 on v3

--- a/solution.py
+++ b/solution.py
@@ -16,6 +16,7 @@
 X_FIRST = (0, 2, 4, 6)
 PARTS = (0, 3, slice(1, 3))
 PLACES = (1, 4, slice(2, 4))
+FAR = (10, 6, 9, 14, 11, 2, 8, 5, 15, 7, 13, 1, 4, 3, 12)
 
 
 def kernel(feat_hbm, w, bias_hbm, out, feat, bias, turned, vol, taps, acc, ready, column,
@@ -111,11 +112,8 @@
         )
 
     def send_feat(g):
-        def send(k, carry):
+        for k in FAR:
             feat_copy(g, k).start()
-            return carry
-
-        lax.fori_loop(1, CHIPS, send, 0)
 
     def wait_feat(g):
         def wait(k, carry):
@@ -179,7 +177,7 @@
             own_taps[i].wait()
             for k in range(1, SIDE):
                 tap_arrived1(i, k).wait()
-            for k in range(1, SIDE):
+            for k in (2, 1, 3):
                 tap_copy2(i, k).start()
 
     def third_phase():
@@ -274,11 +272,8 @@
             ready[z, :, y] = active.reshape(CHIPS, 8, 128).astype(jnp.bfloat16)
         out_own(z).start()
 
-        def send(k, carry):
+        for k in FAR:
             out_copy(z, k).start()
-            return carry
-
-        lax.fori_loop(1, CHIPS, send, 0)
 
     def multiply(unit, first=False, last=False):
         dz, dy = unit // 3, unit % 3

time: 43.9 us -> 43.7 us (level)
  no operation moved by 1% of the time
where the time goes in v4:
time: 43.7 us; the launch traced here: 43.3 us
  Pallas kernels  42.3 us (97%)
  local copies, waits for them, and re-layouts  0.91 us (2%)
    pallas_call x1, Pallas kernels, body(): pl.pallas_call(kernel, out_shape=jax.ShapeDtypeStruct((PLANES, 64, 8, 128...  42.3 us
    transpose x1, local copies, waits for them, and re-layouts, body(): return got.transpose(0, 2, 1, 3)  0.91 us

profile of v4, /device:TPU:2, one launch (start us, length us, event | category | flops | bytes accessed | tf_op | source)
XLA Modules:
  0.0 43.3 jit_solution(10605029360670815451)
XLA Ops:
  0.0 42.3 %shard_map.37 = bf16[4,64,8,128]{3,2,1,0:T(8,128)(2,1)S(1)} custom-call(bf16[4,8,64,128]{3,2,1,0:T(8,128)(2,1)} %feat_hbm.1, bf16[9,3,8,256]{3,2,1,0:T(8,128)(2,1)} %bitcast.3, f32[256]{0:T(256)} %bias_hbm.1), custom_call_target="tpu_custom_call" | custom-call | tf_op jit(solution)/shard_map/pallas_call | solution.py:378
  42.4 0.9 %copy.4 = bf16[4,8,64,128]{3,2,1,0:T(8,128)(2,1)} copy(bf16[4,8,64,128]{3,1,2,0:T(8,128)(2,1)S(1)} %bitcast.2) | data formatting | bytes 1048576 | tf_op jit(solution)/shard_map/transpose | solution.py:405

commit v5 on v4

--- a/solution.py
+++ b/solution.py
@@ -13,7 +13,7 @@
 COUPLES = ((0, 6), (2, 8))
 COMMON = (3, 4, 5, 1, 7)
 OWN = len(COUPLES) + len(COMMON)
-X_FIRST = (0, 2, 4, 6)
+X_FIRST = (1, 3, 5)
 PARTS = (0, 3, slice(1, 3))
 PLACES = (1, 4, slice(2, 4))
 FAR = (10, 6, 9, 14, 11, 2, 8, 5, 15, 7, 13, 1, 4, 3, 12)

time: 43.7 us -> 43.2 us (0.989)
  no operation moved by 1% of the time
where the time goes in v5:
time: 43.2 us; the launch traced here: 43.1 us
  Pallas kernels  42.2 us (98%)
  local copies, waits for them, and re-layouts  0.91 us (2%)
    pallas_call x1, Pallas kernels, body(): pl.pallas_call(kernel, out_shape=jax.ShapeDtypeStruct((PLANES, 64, 8, 128...  42.2 us
    transpose x1, local copies, waits for them, and re-layouts, body(): return got.transpose(0, 2, 1, 3)  0.91 us

profile of v5, /device:TPU:2, one launch (start us, length us, event | category | flops | bytes accessed | tf_op | source)
XLA Modules:
  0.0 43.1 jit_solution(14860418734562668069)
XLA Ops:
  0.0 42.2 %shard_map.37 = bf16[4,64,8,128]{3,2,1,0:T(8,128)(2,1)S(1)} custom-call(bf16[4,8,64,128]{3,2,1,0:T(8,128)(2,1)} %feat_hbm.1, bf16[9,3,8,256]{3,2,1,0:T(8,128)(2,1)} %bitcast.3, f32[256]{0:T(256)} %bias_hbm.1), custom_call_target="tpu_custom_call" | custom-call | tf_op jit(solution)/shard_map/pallas_call | solution.py:378
  42.2 0.9 %copy.4 = bf16[4,8,64,128]{3,2,1,0:T(8,128)(2,1)} copy(bf16[4,8,64,128]{3,1,2,0:T(8,128)(2,1)S(1)} %bitcast.2) | data formatting | bytes 1048576 | tf_op jit(solution)/shard_map/transpose | solution.py:405

commit v6 on v5

--- a/solution.py
+++ b/solution.py
@@ -212,6 +212,7 @@
         for k in range(1, SIDE):
             tap_copy1(i, k).start()
     send_feat(2)
+    second_phase(range(len(COUPLES)))
     own_feat.wait()
     wait_feat(0)
 
@@ -229,7 +230,6 @@
 
     top = across(3, vol.at[:, 4, :, core])
     top.start()
-    second_phase(range(len(COUPLES)))
     second_phase(range(len(COUPLES), OWN))
     wait_feat(2)
     middle = across(4, vol.at[:, 2:4, :, core])

time: 43.2 us -> 43.2 us (level)
  no operation moved by 1% of the time
where the time goes in v6:
time: 43.2 us; the launch traced here: 43.1 us
  Pallas kernels  42.2 us (98%)
  local copies, waits for them, and re-layouts  0.91 us (2%)
    pallas_call x1, Pallas kernels, body(): pl.pallas_call(kernel, out_shape=jax.ShapeDtypeStruct((PLANES, 64, 8, 128...  42.2 us
    transpose x1, local copies, waits for them, and re-layouts, body(): return got.transpose(0, 2, 1, 3)  0.91 us

profile of v6, /device:TPU:2, one launch (start us, length us, event | category | flops | bytes accessed | tf_op | source)
XLA Modules:
  0.0 43.1 jit_solution(5543782720531928507)
XLA Ops:
  0.0 42.2 %shard_map.37 = bf16[4,64,8,128]{3,2,1,0:T(8,128)(2,1)S(1)} custom-call(bf16[4,8,64,128]{3,2,1,0:T(8,128)(2,1)} %feat_hbm.1, bf16[9,3,8,256]{3,2,1,0:T(8,128)(2,1)} %bitcast.3, f32[256]{0:T(256)} %bias_hbm.1), custom_call_target="tpu_custom_call" | custom-call | tf_op jit(solution)/shard_map/pallas_call | solution.py:378
  42.2 0.9 %copy.4 = bf16[4,8,64,128]{3,2,1,0:T(8,128)(2,1)} copy(bf16[4,8,64,128]{3,1,2,0:T(8,128)(2,1)S(1)} %bitcast.2) | data formatting | bytes 1048576 | tf_op jit(solution)/shard_map/transpose | solution.py:405
